TPU v7x, 32 devices: a whole 2x2x4 slice. The times are simulated.
32 devices in a mesh: grp: 2 (over y), pb: 4 (over z), re: 2 (over x), ka: 2 (over core).
Axes of the slice: x: 2, y: 2, z: 4, core: 2. Of those that a mesh axis runs over, the one named last changes fastest.
Arguments:
- g_wann: bfloat16 [2, 1024, 128, 256], P(None, 'pb', ('grp', 're'), 'ka'), parts along dimension 2, may hold values from -0.0234375 to 0.0234375
- phonon_phase: bfloat16 [2, 2048, 1024], P(None, 'pb'), may hold values from -1 to 1, as said below
- electron_phase: bfloat16 [2, 8, 64], replicated, may hold values from -1 to 1, as said below
Outputs:
- coupling: float32 [16, 2, 2048, 256], P(('grp', 're'), None, 'pb', 'ka'), parts along dimension 0
There are 2 independent parts, one for each index of `grp`. A program takes and returns all parts, laid end to end along the dimension named above; an argument that names none is the same for every part. Nothing has to cross between parts.
Inputs may be any that keep to these rules, and one draw needn't show every extreme that they name: `phonon_phase`: entries 0 and 1 along the first dimension are the cosine and sine of one angle. `electron_phase`: entries 0 and 1 along the first dimension are the cosine and sine of one angle.
All inputs are finite; a program needn't handle non-finite values.
Results may differ from a plain program's by a relative error of at most 0.0029.
Values may be sent and summed in bfloat16 or wider, within the bound.
A program may use at most 64 MiB of HBM per device.

v0:
```python
import functools
import jax
import jax.numpy as jnp
from jax import lax
from jax.experimental import pallas as pl
from jax.experimental.pallas import tpu as pltpu
from jax.sharding import PartitionSpec as P

MESH = pl.DeviceIdType.MESH
GROUP = 8
PAIR = 2
UNROLL = 4
AHEAD = 1
SLACK = 0
BF16 = jnp.bfloat16
F32 = jnp.float32


def iota(shape, dim):
    return lax.broadcasted_iota(jnp.int32, shape, dim)


def kernel(
    n_re, n_pb, halves,
    g_hbm, ph_hbm, el_hbm, out,
    g, ph, el_ref, el_block, part, x_first, x_first_recv, x_recv, gath,
    g_sem, ph_sem, el_sem, x_send, x_got, z_send, z_got,
):
    x = lax.axis_index("re")
    z = lax.axis_index("pb")
    k_all, p_loc, width = part.shape
    b = width // 2
    k_own = k_all // n_re
    p_half = p_loc // halves
    e_all = el_ref.shape[2]
    e_loc = g.shape[1] // p_loc
    chunks = k_own * halves
    q_loc = ph.shape[1]

    def g_copy(h):
        rows = pl.ds(h * p_half * e_loc, p_half * e_loc)
        return pltpu.make_async_copy(g_hbm.at[:, rows, :], g.at[:, rows, :], g_sem.at[h])

    barrier = pltpu.get_barrier_semaphore()
    for d in range(1, n_re):
        pl.semaphore_signal(barrier, inc=1, device_id={"re": lax.rem(x + d, n_re)}, device_id_type=MESH)

    @pl.when(z > 0)
    def _():
        pl.semaphore_signal(barrier, inc=1, device_id={"pb": z - 1}, device_id_type=MESH)

    @pl.when(z < n_pb - 1)
    def _():
        pl.semaphore_signal(barrier, inc=1, device_id={"pb": z + 1}, device_id_type=MESH)

    el_copy = pltpu.make_async_copy(el_hbm, el_ref, el_sem)
    el_copy.start()
    for h in range(halves):
        g_copy(h).start()

    rows, cols = k_all * GROUP, GROUP * e_loc
    spread_k = (iota((rows, k_all), 0) // GROUP == iota((rows, k_all), 1)).astype(BF16)
    spread_e = (iota((e_all, cols), 0) == x * e_loc + iota((e_all, cols), 1) % e_loc).astype(BF16)
    same_p = iota((rows, cols), 0) % GROUP == iota((rows, cols), 1) // e_loc

    def spread(table):
        t = jnp.dot(spread_k, table, preferred_element_type=F32).astype(BF16)
        t = jnp.dot(t, spread_e, preferred_element_type=F32)
        return jnp.where(same_p, t, 0.0)

    el_copy.wait()
    cos_e = spread(el_ref[0])
    sin_e = spread(el_ref[1])
    el_block[0:rows, 0:cols] = cos_e.astype(BF16)
    el_block[0:rows, cols:] = (-sin_e).astype(BF16)
    el_block[rows:, 0:cols] = sin_e.astype(BF16)
    el_block[rows:, cols:] = cos_e.astype(BF16)

    def x_first_copy(h, d):
        there = pl.ds(pl.multiple_of(h * p_half, p_half), p_half)
        to = lax.rem(x + d, n_re)
        return pltpu.make_async_remote_copy(
            src_ref=x_first.at[to, there, :],
            dst_ref=x_first_recv.at[d - 1, there, :],
            send_sem=x_send.at[d - 1, h],
            recv_sem=x_got.at[d - 1, h],
            device_id={"re": to},
            device_id_type=MESH,
        )

    def x_copy(c, d):
        k, h = c // halves, c % halves
        there = pl.ds(pl.multiple_of(h * p_half, p_half), p_half)
        to = lax.rem(x + d, n_re)
        return pltpu.make_async_remote_copy(
            src_ref=part.at[to * k_own + k, there, :],
            dst_ref=x_recv.at[d - 1, k, there, :],
            send_sem=x_send.at[d - 1, c],
            recv_sem=x_got.at[d - 1, c],
            device_id={"re": to},
            device_id_type=MESH,
        )

    def z_copy(c, source, way):
        k, h = c // halves, c % halves
        there = pl.ds(pl.multiple_of(source * p_loc + h * p_half, p_half), p_half)
        block = gath.at[k, there, :]
        return pltpu.make_async_remote_copy(
            src_ref=block,
            dst_ref=block,
            send_sem=z_send.at[way, c, source],
            recv_sem=z_got.at[c, source],
            device_id={"pb": z + 1 if way else z - 1},
            device_id_type=MESH,
        )

    def own_step(t):
        k, h = t // halves, t % halves
        there = pl.ds(pl.multiple_of(h * p_half, p_half), p_half)
        mine = pl.ds(pl.multiple_of(z * p_loc + h * p_half, p_half), p_half)

        @pl.when(t < halves)
        def _():
            total = part[x * k_own, there, :]
            for d in range(1, n_re):
                x_first_copy(t, d).wait_recv()
                total = total + x_first_recv[d - 1, there, :].astype(F32)
            gath[0, mine, :] = total.astype(BF16)

        @pl.when(t >= halves)
        def _():
            total = part[x * k_own + k, there, :]
            for d in range(1, n_re):
                x_copy(t, d).wait_recv()
                total = total + x_recv[d - 1, k, there, :]
            gath[k, mine, :] = total.astype(BF16)

        @pl.when(z > 0)
        def _():
            z_copy(t, z, 0).start()

        @pl.when(z < n_pb - 1)
        def _():
            z_copy(t, z, 1).start()

    for h in range(halves):
        g_copy(h).wait()

        @pl.loop(h * (p_half // GROUP // PAIR), (h + 1) * (p_half // GROUP // PAIR), unroll=UNROLL)
        def _(j):
            sides = []
            for side in range(PAIR):
                at = pl.ds(pl.multiple_of((j * PAIR + side) * cols, cols), cols)
                sides.append(jnp.concatenate([g[0, at, :], g[1, at, :]], axis=0))
            both = jnp.concatenate(sides, axis=1)
            res = jnp.dot(el_block[...], both, preferred_element_type=F32)
            for side in range(PAIR):
                p_at = pl.ds(pl.multiple_of((j * PAIR + side) * GROUP, GROUP), GROUP)
                for c in range(2):
                    for k in range(k_all):
                        first = (c * k_all + k) * GROUP
                        part[k, p_at, c * b:(c + 1) * b] = res[first:first + GROUP, side * b:(side + 1) * b]

        if h == 0:
            n_meet = n_re - 1 + jnp.where(z > 0, 1, 0) + jnp.where(z < n_pb - 1, 1, 0)
            pl.semaphore_wait(barrier, n_meet)
        there = pl.ds(h * p_half, p_half)
        for r in range(n_re):
            x_first[r, there, :] = part[r * k_own, there, :].astype(BF16)
        for d in range(1, n_re):
            x_first_copy(h, d).start()
        if h >= halves - AHEAD:
            own_step(h - (halves - AHEAD))
    for c in range(halves, chunks):
        for d in range(1, n_re):
            x_copy(c, d).start()
    ph_copy = pltpu.make_async_copy(ph_hbm, ph, ph_sem)
    ph_copy.start()

    @pl.loop(AHEAD, chunks + (n_pb - 2) * (1 + SLACK))
    def _(t):
        @pl.when(t < chunks)
        def _():
            own_step(t)

        for d in range(1, n_pb - 1):
            c = t - d * (1 + SLACK)
            ok = (c >= 0) & (c < chunks)

            @pl.when(ok & (z - d >= 0) & (z < n_pb - 1))
            def _():
                z_copy(c, z - d, 1).wait_recv()
                z_copy(c, z - d, 1).start()

            @pl.when(ok & (z + d < n_pb) & (z > 0))
            def _():
                z_copy(c, z + d, 0).wait_recv()
                z_copy(c, z + d, 0).start()

    ph_copy.wait()
    q_tile = min(256, q_loc)

    @pl.loop(0, k_own)
    def _(k):
        for h in range(halves):
            for s in range(n_pb):
                @pl.when(((s < z) & (z == n_pb - 1)) | ((s > z) & (z == 0)))
                def _():
                    z_copy(k * halves + h, s, 0).wait_recv()

            spans = [slice(s * p_loc + h * p_half, s * p_loc + (h + 1) * p_half) for s in range(n_pb)]

            @pl.loop(0, q_loc // q_tile)
            def _(i):
                at = pl.ds(pl.multiple_of(i * q_tile, q_tile), q_tile)
                data = jnp.concatenate([gath[k, w, :] for w in spans], axis=0)
                cos_q = jnp.concatenate([ph[0, at, w] for w in spans], axis=1)
                sin_q = jnp.concatenate([ph[1, at, w] for w in spans], axis=1)
                by_cos = jnp.dot(cos_q, data, preferred_element_type=F32)
                by_sin = jnp.dot(sin_q, data, preferred_element_type=F32)
                real = by_cos[:, :b] - by_sin[:, b:]
                imag = by_cos[:, b:] + by_sin[:, :b]
                out[k, 0, at, :] = real if h == 0 else out[k, 0, at, :] + real
                out[k, 1, at, :] = imag if h == 0 else out[k, 1, at, :] + imag

    @pl.loop(0, chunks)
    def _(c):
        for d in range(1, n_re):
            @pl.when(c < halves)
            def _():
                x_first_copy(c, d).wait_send()

            @pl.when(c >= halves)
            def _():
                x_copy(c, d).wait_send()
        for s in range(n_pb):
            @pl.when((s >= z) & (z > 0))
            def _():
                z_copy(c, s, 0).wait_send()

            @pl.when((s <= z) & (z < n_pb - 1))
            def _():
                z_copy(c, s, 1).wait_send()


def body(n_re, n_pb, g_wann, phonon_phase, electron_phase):
    _, p_loc, e_loc, b = g_wann.shape
    _, q_loc, p_all = phonon_phase.shape
    k_all = electron_phase.shape[1]
    k_own = k_all // n_re
    halves = 2
    chunks = k_own * halves
    g = g_wann.reshape(2, p_loc * e_loc, b)
    far = pl.BlockSpec(memory_space=pltpu.HBM)
    near = pl.BlockSpec(memory_space=pltpu.VMEM)
    return pl.pallas_call(
        functools.partial(kernel, n_re, n_pb, halves),
        out_shape=jax.ShapeDtypeStruct((k_own, 2, q_loc, b), F32),
        in_specs=[far, far, far],
        out_specs=near,
        scratch_shapes=[
            pltpu.VMEM(g.shape, BF16),
            pltpu.VMEM(phonon_phase.shape, BF16),
            pltpu.VMEM(electron_phase.shape, BF16),
            pltpu.VMEM((2 * k_all * GROUP, 2 * GROUP * e_loc), BF16),
            pltpu.VMEM((k_all, p_loc, 2 * b), F32),
            pltpu.VMEM((n_re, p_loc, 2 * b), BF16),
            pltpu.VMEM((n_re - 1, p_loc, 2 * b), BF16),
            pltpu.VMEM((n_re - 1, k_own, p_loc, 2 * b), F32),
            pltpu.VMEM((k_own, p_all, 2 * b), BF16),
            pltpu.SemaphoreType.DMA((halves,)),
            pltpu.SemaphoreType.DMA,
            pltpu.SemaphoreType.DMA,
            pltpu.SemaphoreType.DMA((n_re - 1, chunks)),
            pltpu.SemaphoreType.DMA((n_re - 1, chunks)),
            pltpu.SemaphoreType.DMA((2, chunks, n_pb)),
            pltpu.SemaphoreType.DMA((chunks, n_pb)),
        ],
        compiler_params=pltpu.CompilerParams(
            collective_id=0, has_side_effects=True, vmem_limit_bytes=24 * 1024 * 1024
        ),
    )(*(pltpu.with_memory_space_constraint(a, pltpu.HBM) for a in (g, phonon_phase, electron_phase)))


def solution(mesh):
    placed = (P(None, "pb", ("grp", "re"), "ka"), P(None, "pb", None), P())
    return jax.shard_map(
        functools.partial(body, mesh.shape["re"], mesh.shape["pb"]),
        mesh=mesh,
        in_specs=placed,
        out_specs=P(("grp", "re"), None, "pb", "ka"),
        check_vma=False,
    )
```

profile of v0, /device:TPU:0, one launch (start us, length us, event | category | flops | bytes accessed | tf_op | source)
XLA Modules:
  0.0 47.0 jit_solution(971277664012674125)
XLA Ops:
  0.0 45.7 %shard_map.37 = f32[4,2,512,128]{3,2,1,0:T(8,128)S(1)} custom-call(bf16[2,8192,128]{2,1,0:T(8,128)(2,1)} %bitcast.1, bf16[2,512,1024]{2,1,0:T(8,128)(2,1)} %ph_hbm.1, bf16[2,8,64]{2,1,0:T(8,128)(2,1)} %el_hbm.1), custom_call_target="tpu_custom_call" | custom-call | tf_op jit(solution)/shard_map/pallas_call | solution.py:256
  45.7 1.3 %copy.5 = f32[4,2,512,128]{3,2,1,0:T(8,128)} copy(f32[4,2,512,128]{3,2,1,0:T(8,128)S(1)} %shard_map.37) | data formatting | bytes 4194304
where the time goes:
time: 47.2 us; the launch traced here: 47 us
  Pallas kernels  45.7 us (97%)
  local copies, waits for them, and re-layouts  1.32 us (3%)
    pallas_call x1, Pallas kernels, body(): pl.pallas_call(functools.partial(kernel, n_re, n_pb, halves), out_shape=j...  45.7 us
    unnamed x1, local copies, waits for them, and re-layouts  1.32 us

commit v1 on v0

--- a/solution.py
+++ b/solution.py
@@ -12,6 +12,10 @@
 UNROLL = 4
 AHEAD = 1
 SLACK = 0
+EARLY = 3
+OWN_AHEAD = 5
+PIECES = 4
+LAG = 2
 BF16 = jnp.bfloat16
 F32 = jnp.float32
 
@@ -282,10 +286,471 @@
     )(*(pltpu.with_memory_space_constraint(a, pltpu.HBM) for a in (g, phonon_phase, electron_phase)))
 
 
+def fold_kernel(
+    n_re, n_pb, n_grp, n_ka, halves, early, ahead, pieces,
+    g_hbm, ph_hbm, el_hbm, out,
+    g, ph, el_ref, el_block, part, xs, xr, gath, far_ph, s_out, s_in,
+    g_sem, ph_sem, el_sem, x_send, x_got, z_send, z_got, s_send, s_got,
+    e1_send, e1_got, e2_send, e2_got, e3_send, e3_got,
+):
+    x = lax.axis_index("re")
+    y = lax.axis_index("grp")
+    z = lax.axis_index("pb")
+    core = lax.axis_index("ka")
+    chunks, p_loc, b = part.shape
+    half_b = b // 2
+    k_own = chunks // 2
+    k_all = k_own * n_re
+    p_half = p_loc // halves
+    e_all = el_ref.shape[2]
+    e_loc = g.shape[1] // p_loc
+    q_loc = ph.shape[1]
+    p_far = (n_pb - 1) * p_loc
+    last = n_pb - 1
+
+    lower = 2 * z < n_pb
+    is_edge = (z == 0) | (z == last)
+    is_inner = jnp.logical_not(is_edge)
+    edge = jnp.where(lower, 0, last)
+    far_edge = last - edge
+    mate = last - z
+    inward = jnp.where(lower, z + 1, z - 1)
+    outward = jnp.where(lower, z - 1, z + 1)
+    share = q_loc // (n_grp * n_ka)
+    piece = share // pieces
+
+    def g_copy(h):
+        rows = pl.ds(h * p_half * e_loc, p_half * e_loc)
+        return pltpu.make_async_copy(g_hbm.at[:, rows, :], g.at[:, rows, :], g_sem.at[h])
+
+    barrier = pltpu.get_barrier_semaphore()
+    for axis, at, n in (("re", x, n_re), ("grp", y, n_grp), ("ka", core, n_ka)):
+        for d in range(1, n):
+            pl.semaphore_signal(barrier, inc=1, device_id={axis: lax.rem(at + d, n)}, device_id_type=MESH)
+    pl.semaphore_signal(barrier, inc=1, device_id={"pb": inward}, device_id_type=MESH)
+
+    @pl.when(is_inner)
+    def _():
+        pl.semaphore_signal(barrier, inc=1, device_id={"pb": outward}, device_id_type=MESH)
+
+    el_copy = pltpu.make_async_copy(el_hbm, el_ref, el_sem)
+    el_copy.start()
+    for h in range(halves):
+        g_copy(h).start()
+
+    rows, cols = k_all * GROUP, GROUP * e_loc
+    place = iota((rows, k_all), 0) // GROUP
+    owner = lax.rem(x + place // k_own, n_re)
+    spread_k = (owner * k_own + place % k_own == iota((rows, k_all), 1)).astype(BF16)
+    spread_e = (iota((e_all, cols), 0) == x * e_loc + iota((e_all, cols), 1) % e_loc).astype(BF16)
+    same_p = iota((rows, cols), 0) % GROUP == iota((rows, cols), 1) // e_loc
+
+    def spread(table):
+        t = jnp.dot(spread_k, table, preferred_element_type=F32).astype(BF16)
+        t = jnp.dot(t, spread_e, preferred_element_type=F32)
+        return jnp.where(same_p, t, 0.0)
+
+    el_copy.wait()
+    cos_e = spread(el_ref[0])
+    sin_e = spread(el_ref[1])
+    el_block[0:rows, 0:cols] = cos_e.astype(BF16)
+    el_block[0:rows, cols:] = (-sin_e).astype(BF16)
+    el_block[rows:, 0:cols] = sin_e.astype(BF16)
+    el_block[rows:, cols:] = cos_e.astype(BF16)
+
+    def x_copy(c, h, d):
+        there = pl.ds(pl.multiple_of(h * p_half, p_half), p_half)
+        return pltpu.make_async_remote_copy(
+            src_ref=xs.at[d - 1, c, there, :],
+            dst_ref=xr.at[d - 1, c, there, :],
+            send_sem=x_send.at[d - 1, c, h],
+            recv_sem=x_got.at[d - 1, c, h],
+            device_id={"re": lax.rem(x + d, n_re)},
+            device_id_type=MESH,
+        )
+
+    def z_copy(c, source, way):
+        there = pl.ds(pl.multiple_of(source * p_loc, p_loc), p_loc)
+        block = gath.at[c, there, :]
+        return pltpu.make_async_remote_copy(
+            src_ref=block,
+            dst_ref=block,
+            send_sem=z_send.at[way, c, source],
+            recv_sem=z_got.at[c, source],
+            device_id={"pb": outward if way else inward},
+            device_id_type=MESH,
+        )
+
+    def s_copy(c, i, to):
+        at = pl.ds(pl.multiple_of(i * q_tile, q_tile), q_tile)
+        return pltpu.make_async_remote_copy(
+            src_ref=s_out.at[c - early, at, :],
+            dst_ref=s_in.at[c - early, at, :],
+            send_sem=s_send.at[c - early, i],
+            recv_sem=s_got.at[c - early, i],
+            device_id={"pb": to},
+            device_id_type=MESH,
+        )
+
+    def span(of_y, of_core, i):
+        first = (of_y * n_ka + of_core) * share + i * piece
+        return pl.ds(pl.multiple_of(first, piece), piece)
+
+    def e1_copy(i):
+        at = span(y, core, i)
+        wide = pl.ds(pl.multiple_of(jnp.where(lower, p_loc, 0), p_loc), p_far)
+        return pltpu.make_async_remote_copy(
+            src_ref=ph_hbm.at[:, at, wide],
+            dst_ref=far_ph.at[:, at, :],
+            send_sem=e1_send.at[i],
+            recv_sem=e1_got.at[i],
+            device_id={"pb": inward},
+            device_id_type=MESH,
+        )
+
+    def e2_copy(d, i):
+        block = far_ph.at[:, span(y, core, i), :]
+        return pltpu.make_async_remote_copy(
+            src_ref=block,
+            dst_ref=block,
+            send_sem=e2_send.at[d - 1, i],
+            recv_sem=e2_got.at[d - 1, i],
+            device_id={"grp": lax.rem(y + d, n_grp)},
+            device_id_type=MESH,
+        )
+
+    def e3_copy(d, j, i):
+        block = far_ph.at[:, span(lax.rem(y + n_grp - j, n_grp), core, i), :]
+        return pltpu.make_async_remote_copy(
+            src_ref=block,
+            dst_ref=block,
+            send_sem=e3_send.at[d - 1, j, i],
+            recv_sem=e3_got.at[d - 1, j, i],
+            device_id={"ka": lax.rem(core + d, n_ka)},
+            device_id_type=MESH,
+        )
+
+    n_meet = n_re + n_grp + n_ka - 3 + jnp.where(is_edge, 1, 2)
+    pl.semaphore_wait(barrier, n_meet)
+
+    @pl.when(is_edge)
+    def _():
+        for i in range(pieces):
+            e1_copy(i).start()
+
+    left16 = iota((PAIR * GROUP, b), 1) < half_b
+    for h in range(halves):
+        g_copy(h).wait()
+
+        @pl.loop(h * (p_half // GROUP // PAIR), (h + 1) * (p_half // GROUP // PAIR), unroll=UNROLL)
+        def _(j):
+            sides = []
+            for side in range(PAIR):
+                at = pl.ds(pl.multiple_of((j * PAIR + side) * cols, cols), cols)
+                sides.append(jnp.concatenate([g[0, at, :], g[1, at, :]], axis=0))
+            both = jnp.concatenate(sides, axis=1)
+            res = jnp.dot(el_block[...], both, preferred_element_type=F32)
+            p_at = pl.ds(pl.multiple_of(j * PAIR * GROUP, PAIR * GROUP), PAIR * GROUP)
+
+            def piece_of(first):
+                return jnp.concatenate(
+                    [res[first:first + GROUP, s * b:(s + 1) * b] for s in range(PAIR)], axis=0
+                )
+
+            for d in range(n_re):
+                for k in range(k_own):
+                    real = piece_of((d * k_own + k) * GROUP)
+                    imag = piece_of((k_all + d * k_own + k) * GROUP)
+                    one = jnp.where(left16, real, pltpu.roll(imag, half_b, 1))
+                    two = jnp.where(left16, pltpu.roll(real, half_b, 1), imag)
+                    if d == 0:
+                        part[2 * k, p_at, :] = one
+                        part[2 * k + 1, p_at, :] = two
+                    else:
+                        xs[d - 1, 2 * k, p_at, :] = one.astype(BF16)
+                        xs[d - 1, 2 * k + 1, p_at, :] = two.astype(BF16)
+
+        if h < halves - 1:
+            for d in range(1, n_re):
+                x_copy(0, h, d).start()
+    for d in range(1, n_re):
+        x_copy(0, halves - 1, d).start()
+    for c in range(1, chunks):
+        for h in range(halves):
+            for d in range(1, n_re):
+                x_copy(c, h, d).start()
+    ph_copy = pltpu.make_async_copy(ph_hbm, ph, ph_sem)
+    ph_copy.start()
+
+    mine = pl.ds(pl.multiple_of(z * p_loc, p_loc), p_loc)
+
+    def own(c):
+        total = part[c]
+        for d in range(1, n_re):
+            for h in range(halves):
+                x_copy(c, h, d).wait_recv()
+            total = total + xr[d - 1, c].astype(F32)
+        gath[c, mine, :] = total.astype(BF16)
+        z_copy(c, z, 0).start()
+
+        @pl.when(is_inner & (c < early))
+        def _():
+            z_copy(c, z, 1).start()
+
+    def relay_mate(c):
+        @pl.when(is_inner)
+        def _():
+            z_copy(c, mate, 1).wait_recv()
+            z_copy(c, mate, 1).start()
+
+    def pass_piece(i):
+        @pl.when(is_inner)
+        def _():
+            e1_copy(i).wait_recv()
+            for d in range(1, n_grp):
+                e2_copy(d, i).start()
+            for d in range(1, n_ka):
+                e3_copy(d, 0, i).start()
+
+    for t in range(ahead):
+        own(t)
+        if 0 < t <= early:
+            relay_mate(t - 1)
+        if t < pieces:
+            pass_piece(t)
+    for c in range(ahead - 1, early):
+        relay_mate(c)
+    for i in range(ahead, pieces):
+        pass_piece(i)
+
+    @pl.when(is_edge)
+    def _():
+        @pl.loop(ahead, chunks)
+        def _(c):
+            own(c)
+
+    ph_copy.wait()
+    q_tile = min(256, q_loc)
+    tiles = q_loc // q_tile
+    left = iota((q_tile, b), 1) < half_b
+
+    def rotate(by_cos, by_sin):
+        turned = pltpu.roll(by_sin, half_b, 1)
+        return by_cos + jnp.where(left, -turned, turned)
+
+    def fold(c):
+        data = gath[c, pl.ds(pl.multiple_of(jnp.where(lower, p_loc, 0), p_loc), p_far), :]
+
+        @pl.loop(0, tiles)
+        def _(i):
+            at = pl.ds(pl.multiple_of(i * q_tile, q_tile), q_tile)
+            by_cos = jnp.dot(far_ph[0, at, :], data, preferred_element_type=F32)
+            by_sin = jnp.dot(far_ph[1, at, :], data, preferred_element_type=F32)
+            s_out[c - early, at, :] = rotate(by_cos, by_sin).astype(BF16)
+            s_copy(c, i, outward).start()
+
+    def couple(c, cols_at, rows_at):
+        k, s = c // 2, c % 2
+        data = gath[c, rows_at, :]
+
+        @pl.loop(0, tiles)
+        def _(i):
+            at = pl.ds(pl.multiple_of(i * q_tile, q_tile), q_tile)
+            by_cos = jnp.dot(ph[0, at, cols_at], data, preferred_element_type=F32)
+            by_sin = jnp.dot(ph[1, at, cols_at], data, preferred_element_type=F32)
+            out[k, s, at, :] = rotate(by_cos, by_sin)
+
+    def unmix(k):
+        @pl.loop(0, tiles)
+        def _(i):
+            at = pl.ds(pl.multiple_of(i * q_tile, q_tile), q_tile)
+            one = out[k, 0, at, :]
+            two = out[k, 1, at, :]
+            out[k, 0, at, :] = jnp.where(left, one, pltpu.roll(two, half_b, 1))
+            out[k, 1, at, :] = jnp.where(left, pltpu.roll(one, half_b, 1), two)
+
+    @pl.loop(0, chunks + LAG)
+    def _(t):
+        @pl.when(is_inner & (t < chunks))
+        def _():
+            @pl.when(t >= ahead)
+            def _():
+                own(t)
+
+            z_copy(t, edge, 0).wait_recv()
+            z_copy(t, edge, 0).start()
+
+        for i in range(pieces):
+            @pl.when(is_inner & (t == max(0, i - 1)))
+            def _():
+                for j in range(1, n_grp):
+                    e2_copy(j, i).wait_recv()
+                    for d in range(1, n_ka):
+                        e3_copy(d, j, i).start()
+
+        c = t - LAG
+
+        @pl.when(is_inner & (c >= 0) & (c < early))
+        def _():
+            z_copy(c, far_edge, 1).wait_recv()
+            z_copy(c, far_edge, 1).start()
+
+        @pl.when(is_inner & (c == early))
+        def _():
+            for i in range(pieces):
+                for d in range(1, n_ka):
+                    for j in range(n_grp):
+                        e3_copy(d, j, i).wait_recv()
+
+        @pl.when(is_inner & (c >= early))
+        def _():
+            z_copy(c, mate, 1).wait_recv()
+            z_copy(c, far_edge, 1).wait_recv()
+            fold(c)
+
+        @pl.when(is_edge & (c >= 0) & (c < early))
+        def _():
+            z_copy(c, inward, 0).wait_recv()
+            z_copy(c, mate, 0).wait_recv()
+            z_copy(c, jnp.where(lower, 2, last - 2), 0).wait_recv()
+
+        @pl.when((c >= 0) & (is_inner | (c < early)))
+        def _():
+            couple(c, slice(None), slice(None))
+
+            @pl.when(c % 2 == 1)
+            def _():
+                unmix(c // 2)
+
+        @pl.when(is_edge & (c >= early))
+        def _():
+            couple(c, pl.ds(pl.multiple_of(z * p_loc, p_loc), p_loc), mine)
+
+    @pl.when(is_edge)
+    def _():
+        @pl.loop(early, chunks)
+        def _(c):
+            k, s = c // 2, c % 2
+
+            @pl.loop(0, tiles)
+            def _(i):
+                s_copy(c, i, inward).wait_recv()
+                at = pl.ds(pl.multiple_of(i * q_tile, q_tile), q_tile)
+                out[k, s, at, :] = out[k, s, at, :] + s_in[c - early, at, :].astype(F32)
+
+            @pl.when(c % 2 == 1)
+            def _():
+                unmix(k)
+
+        for i in range(pieces):
+            e1_copy(i).wait_send()
+
+    @pl.when(is_inner)
+    def _():
+        for i in range(pieces):
+            for d in range(1, n_grp):
+                e2_copy(d, i).wait_send()
+            for d in range(1, n_ka):
+                for j in range(n_grp):
+                    e3_copy(d, j, i).wait_send()
+
+        @pl.loop(0, chunks)
+        def _(c):
+            z_copy(c, edge, 0).wait_send()
+
+            @pl.when(c < early)
+            def _():
+                z_copy(c, z, 1).wait_send()
+                z_copy(c, mate, 1).wait_send()
+                z_copy(c, far_edge, 1).wait_send()
+
+            @pl.when(c >= early)
+            def _():
+                for i in range(tiles):
+                    s_copy(c, i, outward).wait_send()
+
+    @pl.loop(0, chunks)
+    def _(c):
+        for d in range(1, n_re):
+            for h in range(halves):
+                x_copy(c, h, d).wait_send()
+        z_copy(c, z, 0).wait_send()
+
+
+def fold_body(n_re, n_pb, n_grp, n_ka, g_wann, phonon_phase, electron_phase):
+    _, p_loc, e_loc, b = g_wann.shape
+    _, q_loc, p_all = phonon_phase.shape
+    k_all = electron_phase.shape[1]
+    k_own = k_all // n_re
+    halves = 2
+    chunks = 2 * k_own
+    early = min(EARLY, chunks - 1)
+    ahead = min(OWN_AHEAD, chunks)
+    pieces = PIECES
+    tiles = q_loc // min(256, q_loc)
+    g = g_wann.reshape(2, p_loc * e_loc, b)
+    far = pl.BlockSpec(memory_space=pltpu.HBM)
+    near = pl.BlockSpec(memory_space=pltpu.VMEM)
+    dma = pltpu.SemaphoreType.DMA
+    return pl.pallas_call(
+        functools.partial(fold_kernel, n_re, n_pb, n_grp, n_ka, halves, early, ahead, pieces),
+        out_shape=jax.ShapeDtypeStruct((k_own, 2, q_loc, b), F32),
+        in_specs=[far, far, far],
+        out_specs=near,
+        scratch_shapes=[
+            pltpu.VMEM(g.shape, BF16),
+            pltpu.VMEM(phonon_phase.shape, BF16),
+            pltpu.VMEM(electron_phase.shape, BF16),
+            pltpu.VMEM((2 * k_all * GROUP, 2 * GROUP * e_loc), BF16),
+            pltpu.VMEM((chunks, p_loc, b), F32),
+            pltpu.VMEM((n_re - 1, chunks, p_loc, b), BF16),
+            pltpu.VMEM((n_re - 1, chunks, p_loc, b), BF16),
+            pltpu.VMEM((chunks, p_all, b), BF16),
+            pltpu.VMEM((2, q_loc, (n_pb - 1) * p_loc), BF16),
+            pltpu.VMEM((chunks - early, q_loc, b), BF16),
+            pltpu.VMEM((chunks - early, q_loc, b), BF16),
+            dma((halves,)),
+            dma,
+            dma,
+            dma((n_re - 1, chunks, halves)),
+            dma((n_re - 1, chunks, halves)),
+            dma((2, chunks, n_pb)),
+            dma((chunks, n_pb)),
+            dma((chunks - early, tiles)),
+            dma((chunks - early, tiles)),
+            dma((pieces,)),
+            dma((pieces,)),
+            dma((n_grp - 1, pieces)),
+            dma((n_grp - 1, pieces)),
+            dma((n_ka - 1, n_grp, pieces)),
+            dma((n_ka - 1, n_grp, pieces)),
+        ],
+        compiler_params=pltpu.CompilerParams(
+            collective_id=0, has_side_effects=True, vmem_limit_bytes=32 * 1024 * 1024
+        ),
+    )(*(pltpu.with_memory_space_constraint(a, pltpu.HBM) for a in (g, phonon_phase, electron_phase)))
+
+
+def can_fold(sizes, g_wann, phonon_phase, electron_phase):
+    _, p_loc, _, b = g_wann.shape
+    _, q_loc, _ = phonon_phase.shape
+    n_re, n_pb, n_grp, n_ka = sizes
+    two_inner = n_pb - 2 == 2 and (n_pb - 1) * p_loc > q_loc
+    many = min(n_re, n_grp, n_ka) > 1 and electron_phase.shape[1] // n_re >= 3
+    return two_inner and many and p_loc % b == 0 and q_loc % (16 * PIECES * n_grp * n_ka) == 0
+
+
+def local(sizes, *arrays):
+    if can_fold(sizes, *arrays):
+        return fold_body(*sizes, *arrays)
+    return body(*sizes[:2], *arrays)
+
+
 def solution(mesh):
     placed = (P(None, "pb", ("grp", "re"), "ka"), P(None, "pb", None), P())
+    sizes = tuple(mesh.shape[axis] for axis in ("re", "pb", "grp", "ka"))
     return jax.shard_map(
-        functools.partial(body, mesh.shape["re"], mesh.shape["pb"]),
+        functools.partial(local, sizes),
         mesh=mesh,
         in_specs=placed,
         out_specs=P(("grp", "re"), None, "pb", "ka"),

time: 47.2 us -> 44.6 us (0.945)
  Pallas kernels: 45.7 us -> 43.1 us
    pallas_call x1, Pallas kernels: 45.7 us -> 43.1 us  [fold_body(): pl.pallas_call(functools.partial(fold_kernel, n_re, n_pb, n_grp, n_ka, ha...]
where the time goes in v1:
time: 44.6 us; the launch traced here: 44.4 us
  Pallas kernels  43.1 us (97%)
  local copies, waits for them, and re-layouts  1.32 us (3%)
    pallas_call x1, Pallas kernels, fold_body(): pl.pallas_call(functools.partial(fold_kernel, n_re, n_pb, n_grp, n_ka, ha...  43.1 us
    unnamed x1, local copies, waits for them, and re-layouts  1.32 us

profile of v1, /device:TPU:0, one launch (start us, length us, event | category | flops | bytes accessed | tf_op | source)
XLA Modules:
  0.0 44.4 jit_solution(10008488875231113795)
XLA Ops:
  0.0 43.1 %shard_map.37 = f32[4,2,512,128]{3,2,1,0:T(8,128)S(1)} custom-call(bf16[2,8192,128]{2,1,0:T(8,128)(2,1)} %bitcast.1, bf16[2,512,1024]{2,1,0:T(8,128)(2,1)} %ph_hbm.1, bf16[2,8,64]{2,1,0:T(8,128)(2,1)} %el_hbm.1), custom_call_target="tpu_custom_call" | custom-call | tf_op jit(solution)/shard_map/pallas_call | solution.py:695
  43.1 1.3 %copy.5 = f32[4,2,512,128]{3,2,1,0:T(8,128)} copy(f32[4,2,512,128]{3,2,1,0:T(8,128)S(1)} %shard_map.37) | data formatting | bytes 4194304

commit v2 on v1

--- a/solution.py
+++ b/solution.py
@@ -9,13 +9,15 @@
 MESH = pl.DeviceIdType.MESH
 GROUP = 8
 PAIR = 2
-UNROLL = 4
+UNROLL = 8
 AHEAD = 1
 SLACK = 0
-EARLY = 3
+EARLY = 4
 OWN_AHEAD = 5
 PIECES = 4
+PASS_AT = (0, 1, 2, 3)
 LAG = 2
+SPREAD_AT = (0, 1, 2, 3)
 BF16 = jnp.bfloat16
 F32 = jnp.float32
 
@@ -369,17 +371,30 @@
             device_id_type=MESH,
         )
 
-    def z_copy(c, source, way):
-        there = pl.ds(pl.multiple_of(source * p_loc, p_loc), p_loc)
+    def z_copy(c, h, source, way):
+        there = pl.ds(pl.multiple_of(source * p_loc + h * p_half, p_half), p_half)
         block = gath.at[c, there, :]
         return pltpu.make_async_remote_copy(
             src_ref=block,
             dst_ref=block,
-            send_sem=z_send.at[way, c, source],
-            recv_sem=z_got.at[c, source],
+            send_sem=z_send.at[way, c, h, source],
+            recv_sem=z_got.at[c, h, source],
             device_id={"pb": outward if way else inward},
             device_id_type=MESH,
         )
+
+    def z_got_all(c, source):
+        for h in range(halves):
+            z_copy(c, h, source, 0).wait_recv()
+
+    def z_sent_all(c, source, way):
+        for h in range(halves):
+            z_copy(c, h, source, way).wait_send()
+
+    def z_relay(c, source, way):
+        for h in range(halves):
+            z_copy(c, h, source, way).wait_recv()
+            z_copy(c, h, source, way).start()
 
     def s_copy(c, i, to):
         at = pl.ds(pl.multiple_of(i * q_tile, q_tile), q_tile)
@@ -485,23 +500,24 @@
     mine = pl.ds(pl.multiple_of(z * p_loc, p_loc), p_loc)
 
     def own(c):
-        total = part[c]
-        for d in range(1, n_re):
-            for h in range(halves):
+        for h in range(halves):
+            there = slice(h * p_half, (h + 1) * p_half)
+            total = part[c, there, :]
+            for d in range(1, n_re):
                 x_copy(c, h, d).wait_recv()
-            total = total + xr[d - 1, c].astype(F32)
-        gath[c, mine, :] = total.astype(BF16)
-        z_copy(c, z, 0).start()
-
-        @pl.when(is_inner & (c < early))
-        def _():
-            z_copy(c, z, 1).start()
+                total = total + xr[d - 1, c, there, :].astype(F32)
+            at = pl.ds(pl.multiple_of(z * p_loc + h * p_half, p_half), p_half)
+            gath[c, at, :] = total.astype(BF16)
+            z_copy(c, h, z, 0).start()
+
+            @pl.when(is_inner & (c < early))
+            def _():
+                z_copy(c, h, z, 1).start()
 
     def relay_mate(c):
         @pl.when(is_inner)
         def _():
-            z_copy(c, mate, 1).wait_recv()
-            z_copy(c, mate, 1).start()
+            z_relay(c, mate, 1)
 
     def pass_piece(i):
         @pl.when(is_inner)
@@ -516,12 +532,11 @@
         own(t)
         if 0 < t <= early:
             relay_mate(t - 1)
-        if t < pieces:
-            pass_piece(t)
+        for i in range(pieces):
+            if PASS_AT[i] == t:
+                pass_piece(i)
     for c in range(ahead - 1, early):
         relay_mate(c)
-    for i in range(ahead, pieces):
-        pass_piece(i)
 
     @pl.when(is_edge)
     def _():
@@ -577,11 +592,10 @@
             def _():
                 own(t)
 
-            z_copy(t, edge, 0).wait_recv()
-            z_copy(t, edge, 0).start()
+            z_relay(t, edge, 0)
 
         for i in range(pieces):
-            @pl.when(is_inner & (t == max(0, i - 1)))
+            @pl.when(is_inner & (t == SPREAD_AT[i]))
             def _():
                 for j in range(1, n_grp):
                     e2_copy(j, i).wait_recv()
@@ -592,8 +606,7 @@
 
         @pl.when(is_inner & (c >= 0) & (c < early))
         def _():
-            z_copy(c, far_edge, 1).wait_recv()
-            z_copy(c, far_edge, 1).start()
+            z_relay(c, far_edge, 1)
 
         @pl.when(is_inner & (c == early))
         def _():
@@ -604,15 +617,15 @@
 
         @pl.when(is_inner & (c >= early))
         def _():
-            z_copy(c, mate, 1).wait_recv()
-            z_copy(c, far_edge, 1).wait_recv()
+            z_got_all(c, mate)
+            z_got_all(c, far_edge)
             fold(c)
 
         @pl.when(is_edge & (c >= 0) & (c < early))
         def _():
-            z_copy(c, inward, 0).wait_recv()
-            z_copy(c, mate, 0).wait_recv()
-            z_copy(c, jnp.where(lower, 2, last - 2), 0).wait_recv()
+            z_got_all(c, inward)
+            z_got_all(c, mate)
+            z_got_all(c, jnp.where(lower, 2, last - 2))
 
         @pl.when((c >= 0) & (is_inner | (c < early)))
         def _():
@@ -656,13 +669,13 @@
 
         @pl.loop(0, chunks)
         def _(c):
-            z_copy(c, edge, 0).wait_send()
+            z_sent_all(c, edge, 0)
 
             @pl.when(c < early)
             def _():
-                z_copy(c, z, 1).wait_send()
-                z_copy(c, mate, 1).wait_send()
-                z_copy(c, far_edge, 1).wait_send()
+                z_sent_all(c, z, 1)
+                z_sent_all(c, mate, 1)
+                z_sent_all(c, far_edge, 1)
 
             @pl.when(c >= early)
             def _():
@@ -674,7 +687,7 @@
         for d in range(1, n_re):
             for h in range(halves):
                 x_copy(c, h, d).wait_send()
-        z_copy(c, z, 0).wait_send()
+        z_sent_all(c, z, 0)
 
 
 def fold_body(n_re, n_pb, n_grp, n_ka, g_wann, phonon_phase, electron_phase):
@@ -714,8 +727,8 @@
             dma,
             dma((n_re - 1, chunks, halves)),
             dma((n_re - 1, chunks, halves)),
-            dma((2, chunks, n_pb)),
-            dma((chunks, n_pb)),
+            dma((2, chunks, halves, n_pb)),
+            dma((chunks, halves, n_pb)),
             dma((chunks - early, tiles)),
             dma((chunks - early, tiles)),
             dma((pieces,)),

time: 44.6 us -> 43.1 us (0.966)
  Pallas kernels: 43.1 us -> 41.7 us
    pallas_call x1, Pallas kernels: 43.1 us -> 41.7 us  [fold_body(): pl.pallas_call(functools.partial(fold_kernel, n_re, n_pb, n_grp, n_ka, ha...]
where the time goes in v2:
time: 43.1 us; the launch traced here: 43 us
  Pallas kernels  41.7 us (97%)
  local copies, waits for them, and re-layouts  1.32 us (3%)
    pallas_call x1, Pallas kernels, fold_body(): pl.pallas_call(functools.partial(fold_kernel, n_re, n_pb, n_grp, n_ka, ha...  41.7 us
    unnamed x1, local copies, waits for them, and re-layouts  1.32 us

profile of v2, /device:TPU:0, one launch (start us, length us, event | category | flops | bytes accessed | tf_op | source)
XLA Modules:
  0.0 43.0 jit_solution(7758142673524051452)
XLA Ops:
  0.0 41.7 %shard_map.37 = f32[4,2,512,128]{3,2,1,0:T(8,128)S(1)} custom-call(bf16[2,8192,128]{2,1,0:T(8,128)(2,1)} %bitcast.1, bf16[2,512,1024]{2,1,0:T(8,128)(2,1)} %ph_hbm.1, bf16[2,8,64]{2,1,0:T(8,128)(2,1)} %el_hbm.1), custom_call_target="tpu_custom_call" | custom-call | tf_op jit(solution)/shard_map/pallas_call | solution.py:708
  41.7 1.3 %copy.5 = f32[4,2,512,128]{3,2,1,0:T(8,128)} copy(f32[4,2,512,128]{3,2,1,0:T(8,128)S(1)} %shard_map.37) | data formatting | bytes 4194304
